TPU v7x, 256 devices: a whole 4x4x8 slice. The times are simulated.
256 devices in a mesh: seq: 128 (over x, z, y_lo, core), head: 2 (over y_hi).
Axes of the slice: x: 4, y: 4 (y_hi: 2, y_lo: 2; y = y_hi * 2 + y_lo), z: 8, core: 2. Of those that a mesh axis runs over, the one named last changes fastest.
Arguments:
- queries: bfloat16 [1, 32768, 16, 128], P(None, 'seq', 'head'), may hold values from -6 to 6
- keys: bfloat16 [1, 32768, 4, 128], P(None, 'seq', 'head'), may hold values from -6 to 6
- values: bfloat16 [1, 32768, 4, 128], P(None, 'seq', 'head'), may hold values from -6 to 6
- norm_gain: float32 [16, 128], P('head'), may hold values from 0.25 to 1.75
- out_grad: bfloat16 [1, 32768, 16, 128], P(None, 'seq', 'head'), may hold values from -6 to 6
- window_reach: int32 [1, 128], P(None, 'seq'), may hold values from 0 to 256
- partner_mask: int32 [1, 128, 6], P(None, 'seq'), may hold values 0 or 1
Outputs:
- normed: bfloat16 [1, 32768, 16, 128], P(None, 'seq', 'head')
- query_grad: bfloat16 [1, 32768, 16, 128], P(None, 'seq', 'head')
- key_gradient: bfloat16 [1, 32768, 4, 128], P(None, 'seq', 'head')
- value_gradient: bfloat16 [1, 32768, 4, 128], P(None, 'seq', 'head')
All inputs are finite; a program needn't handle non-finite values. No bound on the sum of `partner_mask` on one device may be relied on, other than what follows from the above.
Results may differ from a plain program's by a relative error of at most 0.029.
Values may be sent and summed in bfloat16 or wider, within the bound.
No kernel may reach another device: no remote copies, remote signals or barrier semaphores. Data moves between devices by JAX's collectives and lax.ppermute only.
A program may use at most 64 MiB of HBM per device.

v0:
```python
import math
import jax
import jax.numpy as jnp
from jax import lax
from jax.sharding import PartitionSpec as P

epsilon = 1e-06


def passed_along(value, axis, steps):
    count = lax.axis_size(axis)
    leading, last = (max(0, -steps), min(count, count - steps))
    return lax.ppermute(value, axis, [(source, source + steps) for source in range(leading, last)])


def per_device(queries, keys, values, norm_gain, out_grad, window_reach, partner_mask):
    batch_size, block_rows, local_heads, head_size = queries.shape
    key_heads = keys.shape[2]
    group_size = local_heads // key_heads
    score_scale = 1.0 / math.sqrt(head_size)
    device_count = lax.axis_size("seq")
    my_block = lax.axis_index("seq")
    level_count = len([level for level in range(1, 11) if 2 ** (level + 1) <= device_count])
    grouped = queries.reshape(batch_size, block_rows, key_heads, group_size, head_size)
    window_pair = passed_along((keys, values), "seq", 1)
    partner_pairs = []
    for level in range(1, level_count + 1):
        partner_pairs.append(passed_along((keys, values), "seq", 2**level))
    query_pos = lax.broadcasted_iota(jnp.int32, (block_rows, block_rows), 0)
    key_pos = lax.broadcasted_iota(jnp.int32, (block_rows, block_rows), 1)
    own_mask = (key_pos <= query_pos)[None, None, None]
    window_mask = (
        (key_pos[None] >= block_rows - window_reach[:, 0][:, None, None]) & (my_block >= 1)
    )[:, None, None]
    block_list = [(keys, values, own_mask), (window_pair[0], window_pair[1], window_mask)]
    for level in range(1, level_count + 1):
        level_on = (partner_mask[:, 0, level - 1] == 1) & (my_block >= 2**level)
        block_list.append(
            (
                partner_pairs[level - 1][0],
                partner_pairs[level - 1][1],
                level_on[:, None, None, None, None],
            )
        )

    def scores_of(key_block, key_mask):
        raw_scores = (
            jnp.einsum("buhgd,bshd->bhgus", grouped, key_block, preferred_element_type=jnp.float32)
            * score_scale
        )
        return jnp.where(key_mask, raw_scores, -jnp.inf)

    score_list = [scores_of(key_block, key_mask) for key_block, value_block, key_mask in block_list]
    running = jnp.max(score_list[0], axis=-1)
    exp_total = jnp.sum(jnp.exp(score_list[0] - running[..., None]), axis=-1)
    for current in score_list[1:]:
        updated = jnp.maximum(running, jnp.max(current, axis=-1))
        exp_total = exp_total * jnp.exp(running - updated) + jnp.sum(
            jnp.exp(current - updated[..., None]), axis=-1
        )
        running = updated
    log_total = running + jnp.log(exp_total)
    weight_list = [jnp.exp(current - log_total[..., None]) for current in score_list]
    prob_list = [weights.astype(jnp.bfloat16) for weights in weight_list]
    accumulated = jnp.zeros(grouped.shape, jnp.float32)
    for entry, probabilities in zip(block_list, prob_list):
        accumulated = accumulated + jnp.einsum(
            "bhgus,bshd->buhgd", probabilities, entry[1], preferred_element_type=jnp.float32
        )
    attention = accumulated.astype(jnp.bfloat16).reshape(
        batch_size, block_rows, local_heads, head_size
    )
    features = local_heads * lax.axis_size("head") * head_size
    attn_wide = attention.astype(jnp.float32)
    square_total = lax.psum(jnp.sum(attn_wide * attn_wide, axis=(2, 3)), "head")
    inverse = lax.rsqrt(square_total / features + epsilon)
    normed = (norm_gain * attn_wide * inverse[..., None, None]).astype(jnp.bfloat16)
    scaled_grad = norm_gain * out_grad.astype(jnp.float32)
    dot_total = lax.psum(jnp.sum(scaled_grad * attn_wide, axis=(2, 3)), "head")
    attention_gradient = (
        scaled_grad * inverse[..., None, None]
        - attn_wide * (dot_total * inverse**3 / features)[..., None, None]
    ).astype(jnp.bfloat16)
    correction_rows = jnp.sum(attention_gradient.astype(jnp.float32) * attn_wide, axis=-1)
    correction_rows = correction_rows.reshape(
        batch_size, block_rows, key_heads, group_size
    ).transpose(0, 2, 3, 1)
    grad_grouped = attention_gradient.reshape(
        batch_size, block_rows, key_heads, group_size, head_size
    )
    query_acc = jnp.zeros(grouped.shape, jnp.float32)
    partials = []
    for entry, weights, probabilities in zip(block_list, weight_list, prob_list):
        key_block, value_block = (entry[0], entry[1])
        prob_grad = jnp.einsum(
            "buhgd,bshd->bhgus", grad_grouped, value_block, preferred_element_type=jnp.float32
        )
        score_grad = (weights * (prob_grad - correction_rows[..., None])).astype(jnp.bfloat16)
        query_acc = query_acc + jnp.einsum(
            "bhgus,bshd->buhgd", score_grad, key_block, preferred_element_type=jnp.float32
        )
        key_part = jnp.einsum(
            "bhgus,buhgd->bshd", score_grad, grouped, preferred_element_type=jnp.float32
        )
        value_part = jnp.einsum(
            "bhgus,buhgd->bshd", probabilities, grad_grouped, preferred_element_type=jnp.float32
        )
        partials.append((key_part, value_part))
    key_sum, value_sum = partials[0]
    nearest = partials[1]
    for level in range(1, level_count + 1):
        level_part = partials[level + 1]
        arrived = (
            passed_along(level_part[0].astype(jnp.bfloat16), "seq", -(2**level)).astype(
                jnp.float32
            ),
            passed_along(level_part[1].astype(jnp.bfloat16), "seq", -(2**level)).astype(
                jnp.float32
            ),
        )
        key_sum = key_sum + arrived[0]
        value_sum = value_sum + arrived[1]
    arrived = (
        passed_along(nearest[0].astype(jnp.bfloat16), "seq", -1).astype(jnp.float32),
        passed_along(nearest[1].astype(jnp.bfloat16), "seq", -1).astype(jnp.float32),
    )
    key_sum = key_sum + arrived[0]
    value_sum = value_sum + arrived[1]
    query_grad = (
        (query_acc * score_scale)
        .astype(jnp.bfloat16)
        .reshape(batch_size, block_rows, local_heads, head_size)
    )
    key_gradient = (key_sum * score_scale).astype(jnp.bfloat16)
    value_gradient = value_sum.astype(jnp.bfloat16)
    return (normed, query_grad, key_gradient, value_gradient)


def solution(mesh):
    return jax.shard_map(
        per_device,
        mesh=mesh,
        in_specs=(
            P(None, "seq", "head", None),
            P(None, "seq", "head", None),
            P(None, "seq", "head", None),
            P("head", None),
            P(None, "seq", "head", None),
            P(None, "seq"),
            P(None, "seq", None),
        ),
        out_specs=(
            P(None, "seq", "head", None),
            P(None, "seq", "head", None),
            P(None, "seq", "head", None),
            P(None, "seq", "head", None),
        ),
        check_vma=False,
    )
```

profile of v0, /device:TPU:227, one launch (start us, length us, event | category | flops | bytes accessed | tf_op | source)
XLA Modules:
  0.0 215.6 jit_solution(11145276876369639496)
XLA Ops:
  2.4 3.7 %collective-permute-start.13 = (bf16[1,256,2,128]{1,3,2,0:T(8,128)(2,1)}, bf16[1,256,2,128]{1,3,2,0:T(8,128)(2,1)S(1)}, u32[]{:S(2)}, u32[]{:S(2)}) collective-permute-start(bf16[1,256,2,128]{1,3,2,0:T(8,128)(2,1)} %copy.222), channel_id=1, source_target_pairs={{0,128},{2,130},{4,132},{6,134},{8,136},{10,138},{12,140},{14,142}... | collective-permute-start | bytes 393224 | tf_op jit(solution)/shard_map/ppermute | solution.py:13
  8.1 2.4 %collective-permute-start.11 = (bf16[1,256,2,128]{1,3,2,0:T(8,128)(2,1)}, bf16[1,256,2,128]{1,3,2,0:T(8,128)(2,1)S(1)}, u32[]{:S(2)}, u32[]{:S(2)}) collective-permute-start(bf16[1,256,2,128]{1,3,2,0:T(8,128)(2,1)} %copy.222), channel_id=1, source_target_pairs={{0,32},{2,34},{4,36},{6,38},{8,40},{10,42},{12,44},{14,46},{16,48}... | collective-permute-start | bytes 393224 | tf_op jit(solution)/shard_map/ppermute | solution.py:13
  10.5 5.2 %collective-permute-start.10 = (bf16[1,256,2,128]{1,3,2,0:T(8,128)(2,1)}, bf16[1,256,2,128]{1,3,2,0:T(8,128)(2,1)}, u32[]{:S(2)}, u32[]{:S(2)}) collective-permute-start(bf16[1,256,2,128]{1,3,2,0:T(8,128)(2,1)} %copy.222), channel_id=1, source_target_pairs={{0,16},{2,18},{4,20},{6,22},{8,24},{10,26},{12,28},{14,30},{16,32}... | collective-permute-start | bytes 393224 | tf_op jit(solution)/shard_map/ppermute | solution.py:13
  16.7 4.6 %collective-permute-start = (bf16[1,256,2,128]{3,1,2,0:T(8,128)(2,1)S(1)}, bf16[1,256,2,128]{3,1,2,0:T(8,128)(2,1)S(1)}, u32[]{:S(2)}, u32[]{:S(2)}) collective-permute-start(bf16[1,256,2,128]{3,1,2,0:T(8,128)(2,1)S(1)} %copy.206), channel_id=1, source_target_pairs={{0,2},{2,4},{4,6},{6,8},{8,10},{10,12},{12,14},{14,16},{16,18},{18... | collective-permute-start | bytes 393224 | tf_op jit(solution)/shard_map/ppermute | solution.py:13
  28.0 2.5 %collective-permute-start.1 = (bf16[1,256,2,128]{3,1,2,0:T(8,128)(2,1)S(1)}, bf16[1,256,2,128]{3,1,2,0:T(8,128)(2,1)S(1)}, u32[]{:S(2)}, u32[]{:S(2)}) collective-permute-start(bf16[1,256,2,128]{3,1,2,0:T(8,128)(2,1)S(1)} %copy.206), channel_id=1, source_target_pairs={{0,4},{2,6},{4,8},{6,10},{8,12},{10,14},{12,16},{14,18},{16,20},{1... | collective-permute-start | bytes 393224 | tf_op jit(solution)/shard_map/ppermute | solution.py:13
  31.0 4.3 %collective-permute-done.1 = bf16[1,256,2,128]{3,1,2,0:T(8,128)(2,1)S(1)} collective-permute-done((bf16[1,256,2,128]{3,1,2,0:T(8,128)(2,1)S(1)}, bf16[1,256,2,128]{3,1,2,0:T(8,128)(2,1)S(1)}, u32[]{:S(2)}, u32[]{:S(2)}) %collective-permute-start.1) | collective-permute-done | bytes 131104 | tf_op jit(solution)/shard_map/ppermute | solution.py:13
  35.3 4.4 %collective-permute-start.2 = (bf16[1,256,2,128]{3,1,2,0:T(8,128)(2,1)S(1)}, bf16[1,256,2,128]{3,1,2,0:T(8,128)(2,1)S(1)}, u32[]{:S(2)}, u32[]{:S(2)}) collective-permute-start(bf16[1,256,2,128]{3,1,2,0:T(8,128)(2,1)S(1)} %copy.206), channel_id=1, source_target_pairs={{0,8},{2,10},{4,12},{6,14},{8,16},{10,18},{12,20},{14,22},{16,24},... | collective-permute-start | bytes 393224 | tf_op jit(solution)/shard_map/ppermute | solution.py:13
  40.2 2.0 collective-permute-done.2
  42.3 2.9 %collective-permute-start.3 = (bf16[1,256,2,128]{3,1,2,0:T(8,128)(2,1)S(1)}, bf16[1,256,2,128]{3,1,2,0:T(8,128)(2,1)S(1)}, u32[]{:S(2)}, u32[]{:S(2)}) collective-permute-start(bf16[1,256,2,128]{3,1,2,0:T(8,128)(2,1)S(1)} %copy.206), channel_id=1, source_target_pairs={{0,16},{2,18},{4,20},{6,22},{8,24},{10,26},{12,28},{14,30},{16,32}... | collective-permute-start | bytes 393224 | tf_op jit(solution)/shard_map/ppermute | solution.py:13
  45.6 5.1 %collective-permute-done.3 = bf16[1,256,2,128]{3,1,2,0:T(8,128)(2,1)S(1)} collective-permute-done((bf16[1,256,2,128]{3,1,2,0:T(8,128)(2,1)S(1)}, bf16[1,256,2,128]{3,1,2,0:T(8,128)(2,1)S(1)}, u32[]{:S(2)}, u32[]{:S(2)}) %collective-permute-start.3) | collective-permute-done | bytes 131104 | tf_op jit(solution)/shard_map/ppermute | solution.py:13
  53.2 9.1 %collective-permute-done.4 = bf16[1,256,2,128]{3,1,2,0:T(8,128)(2,1)S(1)} collective-permute-done((bf16[1,256,2,128]{3,1,2,0:T(8,128)(2,1)S(1)}, bf16[1,256,2,128]{3,1,2,0:T(8,128)(2,1)S(1)}, u32[]{:S(2)}, u32[]{:S(2)}) %collective-permute-start.4) | collective-permute-done | bytes 131104 | tf_op jit(solution)/shard_map/ppermute | solution.py:13
  64.7 3.3 %collective-permute-done.5 = bf16[1,256,2,128]{3,1,2,0:T(8,128)(2,1)S(1)} collective-permute-done((bf16[1,256,2,128]{3,1,2,0:T(8,128)(2,1)S(1)}, bf16[1,256,2,128]{3,1,2,0:T(8,128)(2,1)S(1)}, u32[]{:S(2)}, u32[]{:S(2)}) %collective-permute-start.5) | collective-permute-done | bytes 131104 | tf_op jit(solution)/shard_map/ppermute | solution.py:13
  71.2 6.7 %collective-permute-start.7 = (bf16[1,256,2,128]{1,3,2,0:T(8,128)(2,1)}, bf16[1,256,2,128]{1,3,2,0:T(8,128)(2,1)S(1)}, u32[]{:S(2)}, u32[]{:S(2)}) collective-permute-start(bf16[1,256,2,128]{1,3,2,0:T(8,128)(2,1)} %copy.222), channel_id=1, source_target_pairs={{0,2},{2,4},{4,6},{6,8},{8,10},{10,12},{12,14},{14,16},{16,18},{18... | collective-permute-start | bytes 393224 | tf_op jit(solution)/shard_map/ppermute | solution.py:13
  81.5 12.9 %collective-permute-start.9 = (bf16[1,256,2,128]{1,3,2,0:T(8,128)(2,1)}, bf16[1,256,2,128]{1,3,2,0:T(8,128)(2,1)S(1)}, u32[]{:S(2)}, u32[]{:S(2)}) collective-permute-start(bf16[1,256,2,128]{1,3,2,0:T(8,128)(2,1)} %copy.222), channel_id=1, source_target_pairs={{0,8},{2,10},{4,12},{6,14},{8,16},{10,18},{12,20},{14,22},{16,24},... | collective-permute-start | bytes 393224 | tf_op jit(solution)/shard_map/ppermute | solution.py:13
  96.7 4.4 %collective-permute-start.8 = (bf16[1,256,2,128]{1,3,2,0:T(8,128)(2,1)}, bf16[1,256,2,128]{1,3,2,0:T(8,128)(2,1)S(1)}, u32[]{:S(2)}, u32[]{:S(2)}) collective-permute-start(bf16[1,256,2,128]{1,3,2,0:T(8,128)(2,1)} %copy.222), channel_id=1, source_target_pairs={{0,4},{2,6},{4,8},{6,10},{8,12},{10,14},{12,16},{14,18},{16,20},{1... | collective-permute-start | bytes 393224 | tf_op jit(solution)/shard_map/ppermute | solution.py:13
  107.1 2.6 %copy.236 = f32[1,256,8,128]{3,2,1,0:T(8,128)} copy(f32[1,256,8,128]{1,3,2,0:T(8,128)} %bitcast.792) | data formatting | bytes 2097152 | tf_op jit(solution)/shard_map/convert_element_type | solution.py:74
  109.7 2.8 %multiply_reduce_fusion.1 = f32[256]{0:T(256)} fusion(f32[1,256,8,128]{3,2,1,0:T(8,128)} %copy.236, bf16[1,256,8,128]{3,2,1,0:T(8,128)(2,1)S(1)} %copy-done.19, f32[8,128]{1,0:T(8,128)S(1)} %copy-done.53), kind=kLoop, calls=%fused_computation.162 | loop fusion | flops 1048320 | bytes 1577984 | tf_op jit(solution)/shard_map/reduce_sum | solution.py:79
  112.5 5.9 %all-reduce = (f32[1,256]{1,0:T(1,128)}, f32[1,256]{1,0:T(1,128)}) all-reduce(f32[1,256]{1,0:T(1,128)S(1)} %bitcast.830, f32[1,256]{1,0:T(1,128)} %bitcast.833), channel_id=1, replica_groups=mesh['seq'=128,'head'=2] {'head'}, use_global_device_ids=true, to_apply=%region_17.18 | all-reduce | flops 512 | bytes 4096 | tf_op jit(solution)/shard_map/psum | solution.py:75
  119.2 4.0 %multiply_reduce_fusion = (f32[256,8]{1,0:T(8,128)}, bf16[1,256,8,128]{3,2,1,0:T(8,128)(2,1)}, bf16[1,256,8,128]{3,2,1,0:T(8,128)(2,1)}) fusion(f32[1,256,8,128]{3,2,1,0:T(8,128)} %copy.236, f32[256]{0:T(256)S(1)} %bitcast.831, f32[256]{0:T(256)S(1)} %bitcast.832, bf16[1,256,8,128]{3,2,1,0:T(8,128)(2,1)S(1)} %copy-done.19, f32[8,128]{1,0:T(8,128)S(1)} %copy-done.53), kind=kLoop, calls=%fused_computation.160 | loop fusion | flops 3143680 | bytes 2635776 | tf_op jit(solution)/shard_map/reduce_sum | solution.py:84
  124.6 2.9 %fusion.78 = bf16[1,256,2,128]{1,3,2,0:T(8,128)(2,1)} fusion(bf16[256,2,4,128]{0,3,2,1:T(8,128)(2,1)S(1)} %copy.282, f32[1,2,4,256,256]{3,4,2,1,0:T(8,128)} %copy-done.6, f32[2,4,256]{2,1,0:T(4,128)S(1)} %bitcast.776), kind=kOutput, calls=%fused_computation.136 | convolution fusion | flops 135331840 | bytes 2760704 | tf_op jit(solution)/shard_map/bhgus,buhgd->bshd/dot_general | solution.py:105
  127.5 2.9 %fusion.79 = bf16[1,256,2,128]{1,3,2,0:T(8,128)(2,1)} fusion(bf16[256,2,4,128]{0,3,2,1:T(8,128)(2,1)S(1)} %copy.282, f32[2,256,256,4]{2,1,3,0:T(8,128)} %copy-done.14, f32[2,4,256]{2,1,0:T(4,128)S(1)} %bitcast.777), kind=kOutput, calls=%fused_computation.137 | convolution fusion | flops 135331840 | bytes 2760704 | tf_op jit(solution)/shard_map/bhgus,buhgd->bshd/dot_general | solution.py:105
  148.5 2.1 collective-permute-start.14
  150.6 2.8 %collective-permute-start.21 = (bf16[1,256,2,128]{1,3,2,0:T(8,128)(2,1)S(1)}, bf16[1,256,2,128]{1,3,2,0:T(8,128)(2,1)S(1)}, u32[]{:S(2)}, u32[]{:S(2)}) collective-permute-start(bf16[1,256,2,128]{1,3,2,0:T(8,128)(2,1)S(1)} %copy-done.51), channel_id=1, source_target_pairs={{4,0},{6,2},{8,4},{10,6},{12,8},{14,10},{16,12},{18,14},{20,16},{2... | collective-permute-start | bytes 393224 | tf_op jit(solution)/shard_map/ppermute | solution.py:13
  157.2 2.1 collective-permute-start.16
  166.9 6.8 %collective-permute-start.17 = (bf16[1,256,2,128]{3,1,2,0:T(8,128)(2,1)S(1)}, bf16[1,256,2,128]{3,1,2,0:T(8,128)(2,1)S(1)}, u32[]{:S(2)}, u32[]{:S(2)}) collective-permute-start(bf16[1,256,2,128]{3,1,2,0:T(8,128)(2,1)S(1)} %fusion.88), channel_id=1, source_target_pairs={{32,0},{34,2},{36,4},{38,6},{40,8},{42,10},{44,12},{46,14},{48,16}... | collective-permute-start | bytes 393224 | tf_op jit(solution)/shard_map/ppermute | solution.py:13
  177.0 10.1 %collective-permute-start.20 = (bf16[1,256,2,128]{3,1,2,0:T(8,128)(2,1)S(1)}, bf16[1,256,2,128]{3,1,2,0:T(8,128)(2,1)S(1)}, u32[]{:S(2)}, u32[]{:S(2)}) collective-permute-start(bf16[1,256,2,128]{3,1,2,0:T(8,128)(2,1)S(1)} %fusion.85), channel_id=1, source_target_pairs={{2,0},{4,2},{6,4},{8,6},{10,8},{12,10},{14,12},{16,14},{18,16},{20... | collective-permute-start | bytes 393224 | tf_op jit(solution)/shard_map/ppermute | solution.py:13
  187.6 4.1 %collective-permute-start.23 = (bf16[1,256,2,128]{1,3,2,0:T(8,128)(2,1)S(1)}, bf16[1,256,2,128]{1,3,2,0:T(8,128)(2,1)S(1)}, u32[]{:S(2)}, u32[]{:S(2)}) collective-permute-start(bf16[1,256,2,128]{1,3,2,0:T(8,128)(2,1)S(1)} %fusion.82), channel_id=1, source_target_pairs={{16,0},{18,2},{20,4},{22,6},{24,8},{26,10},{28,12},{30,14},{32,16}... | collective-permute-start | bytes 393224 | tf_op jit(solution)/shard_map/ppermute | solution.py:13
  191.7 1.9 collective-permute-start.24
  196.9 2.2 %collective-permute-start.27 = (bf16[1,256,2,128]{1,3,2,0:T(8,128)(2,1)S(1)}, bf16[1,256,2,128]{1,3,2,0:T(8,128)(2,1)S(1)}, u32[]{:S(2)}, u32[]{:S(2)}) collective-permute-start(bf16[1,256,2,128]{1,3,2,0:T(8,128)(2,1)S(1)} %copy-done.46), channel_id=1, source_target_pairs={{2,0},{4,2},{6,4},{8,6},{10,8},{12,10},{14,12},{16,14},{18,16},{20... | collective-permute-start | bytes 393224 | tf_op jit(solution)/shard_map/ppermute | solution.py:13
  200.9 5.2 %collective-permute-done.24 = bf16[1,256,2,128]{1,3,2,0:T(8,128)(2,1)S(1)} collective-permute-done((bf16[1,256,2,128]{1,3,2,0:T(8,128)(2,1)S(1)}, bf16[1,256,2,128]{1,3,2,0:T(8,128)(2,1)S(1)}, u32[]{:S(2)}, u32[]{:S(2)}) %collective-permute-start.24) | collective-permute-done | bytes 131104 | tf_op jit(solution)/shard_map/ppermute | solution.py:13
  206.2 2.1 collective-permute-done.25
  208.3 5.9 %collective-permute-done.26 = bf16[1,256,2,128]{1,3,2,0:T(8,128)(2,1)S(1)} collective-permute-done((bf16[1,256,2,128]{1,3,2,0:T(8,128)(2,1)S(1)}, bf16[1,256,2,128]{1,3,2,0:T(8,128)(2,1)S(1)}, u32[]{:S(2)}, u32[]{:S(2)}) %collective-permute-start.26) | collective-permute-done | bytes 131104 | tf_op jit(solution)/shard_map/ppermute | solution.py:13
  (203 shorter events, 69.2 us)
Async XLA Ops:
  2.4 101.7 %collective-permute-start.13 = (bf16[1,256,2,128]{1,3,2,0:T(8,128)(2,1)}, bf16[1,256,2,128]{1,3,2,0:T(8,128)(2,1)S(1)}, u32[]{:S(2)}, u32[]{:S(2)}) collective-permute-start(bf16[1,256,2,128]{1,3,2,0:T(8,128)(2,1)} %copy.222), channel_id=1, source_target_pairs={{0,128},{2,130},{4,132},{6,134},{8,136},{10,138},{12,140},{14,142}... | collective-permute-start | bytes 393224 | tf_op jit(solution)/shard_map/ppermute | solution.py:13
  6.2 97.4 %collective-permute-start.12 = (bf16[1,256,2,128]{1,3,2,0:T(8,128)(2,1)}, bf16[1,256,2,128]{1,3,2,0:T(8,128)(2,1)S(1)}, u32[]{:S(2)}, u32[]{:S(2)}) collective-permute-start(bf16[1,256,2,128]{1,3,2,0:T(8,128)(2,1)} %copy.222), channel_id=1, source_target_pairs={{0,64},{2,66},{4,68},{6,70},{8,72},{10,74},{12,76},{14,78},{16,80}... | collective-permute-start | bytes 393224 | tf_op jit(solution)/shard_map/ppermute | solution.py:13
  8.1 94.9 %collective-permute-start.11 = (bf16[1,256,2,128]{1,3,2,0:T(8,128)(2,1)}, bf16[1,256,2,128]{1,3,2,0:T(8,128)(2,1)S(1)}, u32[]{:S(2)}, u32[]{:S(2)}) collective-permute-start(bf16[1,256,2,128]{1,3,2,0:T(8,128)(2,1)} %copy.222), channel_id=1, source_target_pairs={{0,32},{2,34},{4,36},{6,38},{8,40},{10,42},{12,44},{14,46},{16,48}... | collective-permute-start | bytes 393224 | tf_op jit(solution)/shard_map/ppermute | solution.py:13
  10.5 91.1 %collective-permute-start.10 = (bf16[1,256,2,128]{1,3,2,0:T(8,128)(2,1)}, bf16[1,256,2,128]{1,3,2,0:T(8,128)(2,1)}, u32[]{:S(2)}, u32[]{:S(2)}) collective-permute-start(bf16[1,256,2,128]{1,3,2,0:T(8,128)(2,1)} %copy.222), channel_id=1, source_target_pairs={{0,16},{2,18},{4,20},{6,22},{8,24},{10,26},{12,28},{14,30},{16,32}... | collective-permute-start | bytes 393224 | tf_op jit(solution)/shard_map/ppermute | solution.py:13
  16.7 11.3 %collective-permute-start = (bf16[1,256,2,128]{3,1,2,0:T(8,128)(2,1)S(1)}, bf16[1,256,2,128]{3,1,2,0:T(8,128)(2,1)S(1)}, u32[]{:S(2)}, u32[]{:S(2)}) collective-permute-start(bf16[1,256,2,128]{3,1,2,0:T(8,128)(2,1)S(1)} %copy.206), channel_id=1, source_target_pairs={{0,2},{2,4},{4,6},{6,8},{8,10},{10,12},{12,14},{14,16},{16,18},{18... | collective-permute-start | bytes 393224 | tf_op jit(solution)/shard_map/ppermute | solution.py:13
  22.8 55.7 %copy-start.44 = (f32[2,4,256]{2,1,0:T(4,128)}, f32[2,4,256]{2,1,0:T(4,128)S(1)}, u32[]{:S(2)}) copy-start(f32[2,4,256]{2,1,0:T(4,128)S(1)} %get-tuple-element.48) | copy-start | bytes 24580
  28.0 7.3 %collective-permute-start.1 = (bf16[1,256,2,128]{3,1,2,0:T(8,128)(2,1)S(1)}, bf16[1,256,2,128]{3,1,2,0:T(8,128)(2,1)S(1)}, u32[]{:S(2)}, u32[]{:S(2)}) collective-permute-start(bf16[1,256,2,128]{3,1,2,0:T(8,128)(2,1)S(1)} %copy.206), channel_id=1, source_target_pairs={{0,4},{2,6},{4,8},{6,10},{8,12},{10,14},{12,16},{14,18},{16,20},{1... | collective-permute-start | bytes 393224 | tf_op jit(solution)/shard_map/ppermute | solution.py:13
  31.0 63.4 %copy-start.6 = (f32[1,2,4,256,256]{3,4,2,1,0:T(8,128)}, f32[1,2,4,256,256]{3,4,2,1,0:T(8,128)S(1)}, u32[]{:S(2)}) copy-start(f32[1,2,4,256,256]{3,4,2,1,0:T(8,128)S(1)} %get-tuple-element.51) | copy-start | bytes 6291460
  35.3 7.0 %collective-permute-start.2 = (bf16[1,256,2,128]{3,1,2,0:T(8,128)(2,1)S(1)}, bf16[1,256,2,128]{3,1,2,0:T(8,128)(2,1)S(1)}, u32[]{:S(2)}, u32[]{:S(2)}) collective-permute-start(bf16[1,256,2,128]{3,1,2,0:T(8,128)(2,1)S(1)} %copy.206), channel_id=1, source_target_pairs={{0,8},{2,10},{4,12},{6,14},{8,16},{10,18},{12,20},{14,22},{16,24},... | collective-permute-start | bytes 393224 | tf_op jit(solution)/shard_map/ppermute | solution.py:13
  40.2 64.5 %copy-start.16 = (f32[2,256,256,4]{2,1,3,0:T(8,128)}, f32[2,256,256,4]{2,1,3,0:T(8,128)S(1)}, u32[]{:S(2)}) copy-start(f32[2,256,256,4]{2,1,3,0:T(8,128)S(1)} %get-tuple-element.47) | copy-start | bytes 6291460
  42.3 8.5 %collective-permute-start.3 = (bf16[1,256,2,128]{3,1,2,0:T(8,128)(2,1)S(1)}, bf16[1,256,2,128]{3,1,2,0:T(8,128)(2,1)S(1)}, u32[]{:S(2)}, u32[]{:S(2)}) collective-permute-start(bf16[1,256,2,128]{3,1,2,0:T(8,128)(2,1)S(1)} %copy.206), channel_id=1, source_target_pairs={{0,16},{2,18},{4,20},{6,22},{8,24},{10,26},{12,28},{14,30},{16,32}... | collective-permute-start | bytes 393224 | tf_op jit(solution)/shard_map/ppermute | solution.py:13
  45.6 55.4 %copy-start.8 = (f32[2,256,256,4]{2,1,3,0:T(8,128)}, f32[2,256,256,4]{2,1,3,0:T(8,128)S(1)}, u32[]{:S(2)}) copy-start(f32[2,256,256,4]{2,1,3,0:T(8,128)S(1)} %get-tuple-element.45) | copy-start | bytes 6291460
  50.8 11.5 %collective-permute-start.4 = (bf16[1,256,2,128]{3,1,2,0:T(8,128)(2,1)S(1)}, bf16[1,256,2,128]{3,1,2,0:T(8,128)(2,1)S(1)}, u32[]{:S(2)}, u32[]{:S(2)}) collective-permute-start(bf16[1,256,2,128]{3,1,2,0:T(8,128)(2,1)S(1)} %copy.206), channel_id=1, source_target_pairs={{0,32},{2,34},{4,36},{6,38},{8,40},{10,42},{12,44},{14,46},{16,48}... | collective-permute-start | bytes 393224 | tf_op jit(solution)/shard_map/ppermute | solution.py:13
  62.3 5.7 %collective-permute-start.5 = (bf16[1,256,2,128]{3,1,2,0:T(8,128)(2,1)S(1)}, bf16[1,256,2,128]{3,1,2,0:T(8,128)(2,1)S(1)}, u32[]{:S(2)}, u32[]{:S(2)}) collective-permute-start(bf16[1,256,2,128]{3,1,2,0:T(8,128)(2,1)S(1)} %copy.206), channel_id=1, source_target_pairs={{0,64},{2,66},{4,68},{6,70},{8,72},{10,74},{12,76},{14,78},{16,80}... | collective-permute-start | bytes 393224 | tf_op jit(solution)/shard_map/ppermute | solution.py:13
  68.0 3.2 %collective-permute-start.6 = (bf16[1,256,2,128]{3,1,2,0:T(8,128)(2,1)S(1)}, bf16[1,256,2,128]{3,1,2,0:T(8,128)(2,1)S(1)}, u32[]{:S(2)}, u32[]{:S(2)}) collective-permute-start(bf16[1,256,2,128]{3,1,2,0:T(8,128)(2,1)S(1)} %copy.206), channel_id=1, source_target_pairs={{0,128},{2,130},{4,132},{6,134},{8,136},{10,138},{12,140},{14,142}... | collective-permute-start | bytes 393224 | tf_op jit(solution)/shard_map/ppermute | solution.py:13
  71.2 10.3 %collective-permute-start.7 = (bf16[1,256,2,128]{1,3,2,0:T(8,128)(2,1)}, bf16[1,256,2,128]{1,3,2,0:T(8,128)(2,1)S(1)}, u32[]{:S(2)}, u32[]{:S(2)}) collective-permute-start(bf16[1,256,2,128]{1,3,2,0:T(8,128)(2,1)} %copy.222), channel_id=1, source_target_pairs={{0,2},{2,4},{4,6},{6,8},{8,10},{10,12},{12,14},{14,16},{16,18},{18... | collective-permute-start | bytes 393224 | tf_op jit(solution)/shard_map/ppermute | solution.py:13
  81.5 15.2 %collective-permute-start.9 = (bf16[1,256,2,128]{1,3,2,0:T(8,128)(2,1)}, bf16[1,256,2,128]{1,3,2,0:T(8,128)(2,1)S(1)}, u32[]{:S(2)}, u32[]{:S(2)}) collective-permute-start(bf16[1,256,2,128]{1,3,2,0:T(8,128)(2,1)} %copy.222), channel_id=1, source_target_pairs={{0,8},{2,10},{4,12},{6,14},{8,16},{10,18},{12,20},{14,22},{16,24},... | collective-permute-start | bytes 393224 | tf_op jit(solution)/shard_map/ppermute | solution.py:13
  96.7 8.0 %collective-permute-start.8 = (bf16[1,256,2,128]{1,3,2,0:T(8,128)(2,1)}, bf16[1,256,2,128]{1,3,2,0:T(8,128)(2,1)S(1)}, u32[]{:S(2)}, u32[]{:S(2)}) collective-permute-start(bf16[1,256,2,128]{1,3,2,0:T(8,128)(2,1)} %copy.222), channel_id=1, source_target_pairs={{0,4},{2,6},{4,8},{6,10},{8,12},{10,14},{12,16},{14,18},{16,20},{1... | collective-permute-start | bytes 393224 | tf_op jit(solution)/shard_map/ppermute | solution.py:13
  148.5 18.4 %collective-permute-start.14 = (bf16[1,256,2,128]{3,1,2,0:T(8,128)(2,1)S(1)}, bf16[1,256,2,128]{3,1,2,0:T(8,128)(2,1)S(1)}, u32[]{:S(2)}, u32[]{:S(2)}) collective-permute-start(bf16[1,256,2,128]{3,1,2,0:T(8,128)(2,1)S(1)} %fusion.91), channel_id=1, source_target_pairs={{4,0},{6,2},{8,4},{10,6},{12,8},{14,10},{16,12},{18,14},{20,16},{2... | collective-permute-start | bytes 393224 | tf_op jit(solution)/shard_map/ppermute | solution.py:13
  150.6 23.2 %collective-permute-start.21 = (bf16[1,256,2,128]{1,3,2,0:T(8,128)(2,1)S(1)}, bf16[1,256,2,128]{1,3,2,0:T(8,128)(2,1)S(1)}, u32[]{:S(2)}, u32[]{:S(2)}) collective-permute-start(bf16[1,256,2,128]{1,3,2,0:T(8,128)(2,1)S(1)} %copy-done.51), channel_id=1, source_target_pairs={{4,0},{6,2},{8,4},{10,6},{12,8},{14,10},{16,12},{18,14},{20,16},{2... | collective-permute-start | bytes 393224 | tf_op jit(solution)/shard_map/ppermute | solution.py:13
  153.3 22.3 %collective-permute-start.15 = (bf16[1,256,2,128]{3,1,2,0:T(8,128)(2,1)S(1)}, bf16[1,256,2,128]{3,1,2,0:T(8,128)(2,1)S(1)}, u32[]{:S(2)}, u32[]{:S(2)}) collective-permute-start(bf16[1,256,2,128]{3,1,2,0:T(8,128)(2,1)S(1)} %fusion.90), channel_id=1, source_target_pairs={{8,0},{10,2},{12,4},{14,6},{16,8},{18,10},{20,12},{22,14},{24,16},... | collective-permute-start | bytes 393224 | tf_op jit(solution)/shard_map/ppermute | solution.py:13
  155.3 21.7 %collective-permute-start.22 = (bf16[1,256,2,128]{1,3,2,0:T(8,128)(2,1)S(1)}, bf16[1,256,2,128]{1,3,2,0:T(8,128)(2,1)S(1)}, u32[]{:S(2)}, u32[]{:S(2)}) collective-permute-start(bf16[1,256,2,128]{1,3,2,0:T(8,128)(2,1)S(1)} %copy-done.50), channel_id=1, source_target_pairs={{8,0},{10,2},{12,4},{14,6},{16,8},{18,10},{20,12},{22,14},{24,16},... | collective-permute-start | bytes 393224 | tf_op jit(solution)/shard_map/ppermute | solution.py:13
  157.2 30.4 %collective-permute-start.16 = (bf16[1,256,2,128]{3,1,2,0:T(8,128)(2,1)S(1)}, bf16[1,256,2,128]{3,1,2,0:T(8,128)(2,1)S(1)}, u32[]{:S(2)}, u32[]{:S(2)}) collective-permute-start(bf16[1,256,2,128]{3,1,2,0:T(8,128)(2,1)S(1)} %fusion.89), channel_id=1, source_target_pairs={{16,0},{18,2},{20,4},{22,6},{24,8},{26,10},{28,12},{30,14},{32,16}... | collective-permute-start | bytes 393224 | tf_op jit(solution)/shard_map/ppermute | solution.py:13
  166.9 24.8 %collective-permute-start.17 = (bf16[1,256,2,128]{3,1,2,0:T(8,128)(2,1)S(1)}, bf16[1,256,2,128]{3,1,2,0:T(8,128)(2,1)S(1)}, u32[]{:S(2)}, u32[]{:S(2)}) collective-permute-start(bf16[1,256,2,128]{3,1,2,0:T(8,128)(2,1)S(1)} %fusion.88), channel_id=1, source_target_pairs={{32,0},{34,2},{36,4},{38,6},{40,8},{42,10},{44,12},{46,14},{48,16}... | collective-permute-start | bytes 393224 | tf_op jit(solution)/shard_map/ppermute | solution.py:13
  173.7 19.9 %collective-permute-start.18 = (bf16[1,256,2,128]{3,1,2,0:T(8,128)(2,1)S(1)}, bf16[1,256,2,128]{3,1,2,0:T(8,128)(2,1)S(1)}, u32[]{:S(2)}, u32[]{:S(2)}) collective-permute-start(bf16[1,256,2,128]{3,1,2,0:T(8,128)(2,1)S(1)} %fusion.87), channel_id=1, source_target_pairs={{64,0},{66,2},{68,4},{70,6},{72,8},{74,10},{76,12},{78,14},{80,16}... | collective-permute-start | bytes 393224 | tf_op jit(solution)/shard_map/ppermute | solution.py:13
  175.7 19.9 %collective-permute-start.19 = (bf16[1,256,2,128]{3,1,2,0:T(8,128)(2,1)S(1)}, bf16[1,256,2,128]{3,1,2,0:T(8,128)(2,1)S(1)}, u32[]{:S(2)}, u32[]{:S(2)}) collective-permute-start(bf16[1,256,2,128]{3,1,2,0:T(8,128)(2,1)S(1)} %fusion.86), channel_id=1, source_target_pairs={{128,0},{130,2},{132,4},{134,6},{136,8},{138,10},{140,12},{142,14}... | collective-permute-start | bytes 393224 | tf_op jit(solution)/shard_map/ppermute | solution.py:13
  177.0 19.9 %collective-permute-start.20 = (bf16[1,256,2,128]{3,1,2,0:T(8,128)(2,1)S(1)}, bf16[1,256,2,128]{3,1,2,0:T(8,128)(2,1)S(1)}, u32[]{:S(2)}, u32[]{:S(2)}) collective-permute-start(bf16[1,256,2,128]{3,1,2,0:T(8,128)(2,1)S(1)} %fusion.85), channel_id=1, source_target_pairs={{2,0},{4,2},{6,4},{8,6},{10,8},{12,10},{14,12},{16,14},{18,16},{20... | collective-permute-start | bytes 393224 | tf_op jit(solution)/shard_map/ppermute | solution.py:13
  187.6 13.3 %collective-permute-start.23 = (bf16[1,256,2,128]{1,3,2,0:T(8,128)(2,1)S(1)}, bf16[1,256,2,128]{1,3,2,0:T(8,128)(2,1)S(1)}, u32[]{:S(2)}, u32[]{:S(2)}) collective-permute-start(bf16[1,256,2,128]{1,3,2,0:T(8,128)(2,1)S(1)} %fusion.82), channel_id=1, source_target_pairs={{16,0},{18,2},{20,4},{22,6},{24,8},{26,10},{28,12},{30,14},{32,16}... | collective-permute-start | bytes 393224 | tf_op jit(solution)/shard_map/ppermute | solution.py:13
  191.7 14.4 %collective-permute-start.24 = (bf16[1,256,2,128]{1,3,2,0:T(8,128)(2,1)S(1)}, bf16[1,256,2,128]{1,3,2,0:T(8,128)(2,1)S(1)}, u32[]{:S(2)}, u32[]{:S(2)}) collective-permute-start(bf16[1,256,2,128]{1,3,2,0:T(8,128)(2,1)S(1)} %copy-done.49), channel_id=1, source_target_pairs={{32,0},{34,2},{36,4},{38,6},{40,8},{42,10},{44,12},{46,14},{48,16}... | collective-permute-start | bytes 393224 | tf_op jit(solution)/shard_map/ppermute | solution.py:13
  193.7 14.6 %collective-permute-start.25 = (bf16[1,256,2,128]{1,3,2,0:T(8,128)(2,1)S(1)}, bf16[1,256,2,128]{1,3,2,0:T(8,128)(2,1)S(1)}, u32[]{:S(2)}, u32[]{:S(2)}) collective-permute-start(bf16[1,256,2,128]{1,3,2,0:T(8,128)(2,1)S(1)} %copy-done.48), channel_id=1, source_target_pairs={{64,0},{66,2},{68,4},{70,6},{72,8},{74,10},{76,12},{78,14},{80,16}... | collective-permute-start | bytes 393224 | tf_op jit(solution)/shard_map/ppermute | solution.py:13
  195.6 18.6 %collective-permute-start.26 = (bf16[1,256,2,128]{1,3,2,0:T(8,128)(2,1)S(1)}, bf16[1,256,2,128]{1,3,2,0:T(8,128)(2,1)S(1)}, u32[]{:S(2)}, u32[]{:S(2)}) collective-permute-start(bf16[1,256,2,128]{1,3,2,0:T(8,128)(2,1)S(1)} %copy-done.47), channel_id=1, source_target_pairs={{128,0},{130,2},{132,4},{134,6},{136,8},{138,10},{140,12},{142,14}... | collective-permute-start | bytes 393224 | tf_op jit(solution)/shard_map/ppermute | solution.py:13
  196.9 17.3 %collective-permute-start.27 = (bf16[1,256,2,128]{1,3,2,0:T(8,128)(2,1)S(1)}, bf16[1,256,2,128]{1,3,2,0:T(8,128)(2,1)S(1)}, u32[]{:S(2)}, u32[]{:S(2)}) collective-permute-start(bf16[1,256,2,128]{1,3,2,0:T(8,128)(2,1)S(1)} %copy-done.46), channel_id=1, source_target_pairs={{2,0},{4,2},{6,4},{8,6},{10,8},{12,10},{14,12},{16,14},{18,16},{20... | collective-permute-start | bytes 393224 | tf_op jit(solution)/shard_map/ppermute | solution.py:13
  (50 other events, 493.9 us)
where the time goes:
time: 217 us; the launch traced here: 216 us
  starting transfers between devices  99.2 us (46%)
  waiting for transfers between devices  40.8 us (19%)
  matrix products  36 us (17%)
  local copies, waits for them, and re-layouts  17.3 us (8%)
  other arithmetic  10.1 us (5%)
  between operations  6.14 us (3%)
  blocking collectives  5.95 us (3%)
    ppermute x28, starting transfers between devices, passed_along(): lax.ppermute(value, axis, [(source, source + steps) for source in range(l...  99.2 us
    ppermute x28, waiting for transfers between devices, passed_along(): lax.ppermute(value, axis, [(source, source + steps) for source in range(l...  40.8 us
    dot_general x8, matrix products, per_device(): jnp.einsum('bhgus,buhgd->bshd', probabilities, grad_grouped, preferred_el...  11.6 us
    unnamed x113, local copies, waits for them, and re-layouts  10.4 us
    dot_general x8, matrix products, per_device(): jnp.einsum('bhgus,bshd->buhgd', probabilities, entry[1], preferred_elemen...  6.06 us
    psum x1, blocking collectives, per_device(): square_total = lax.psum(jnp.sum(attn_wide * attn_wide, axis=(2, 3)), 'head')  5.95 us
    dot_general x8, matrix products, per_device(): jnp.einsum('buhgd,bshd->bhgus', grad_grouped, value_block, preferred_elem...  5.82 us
    dot_general x8, matrix products, scores_of(): jnp.einsum('buhgd,bshd->bhgus', grouped, key_block, preferred_element_typ...  4.65 us
  transfers between devices with their start and end apart: 28, of which 11 were waited for; matrix products, arithmetic and copies ran while one was open for 10% of the time, Pallas kernels for 0%

commit v1 on v0

--- a/solution.py
+++ b/solution.py
@@ -72,7 +72,9 @@
     )
     features = local_heads * lax.axis_size("head") * head_size
     attn_wide = attention.astype(jnp.float32)
-    square_total = lax.psum(jnp.sum(attn_wide * attn_wide, axis=(2, 3)), "head")
+    square_total = jnp.sum(
+        lax.all_gather(jnp.sum(attn_wide * attn_wide, axis=(2, 3)), "head"), axis=0
+    )
     inverse = lax.rsqrt(square_total / features + epsilon)
     normed = (norm_gain * attn_wide * inverse[..., None, None]).astype(jnp.bfloat16)
     scaled_grad = norm_gain * out_grad.astype(jnp.float32)

time: 217 us -> 224 us (1.032)
  blocking collectives: 5.95 us -> 10.8 us
    all_gather x0 -> x1, blocking collectives: none -> 4.79 us  [per_device(): lax.all_gather(jnp.sum(attn_wide * attn_wide, axis=(2, 3)), 'head')]
where the time goes in v1:
time: 224 us; the launch traced here: 223 us
  starting transfers between devices  101 us (45%)
  waiting for transfers between devices  40.5 us (18%)
  matrix products  36.6 us (16%)
  local copies, waits for them, and re-layouts  17.3 us (8%)
  other arithmetic  10.8 us (5%)
  blocking collectives  10.8 us (5%)
  between operations  6.23 us (3%)
    ppermute x28, starting transfers between devices, passed_along(): lax.ppermute(value, axis, [(source, source + steps) for source in range(l...  101 us
    ppermute x28, waiting for transfers between devices, passed_along(): lax.ppermute(value, axis, [(source, source + steps) for source in range(l...  40.5 us
    dot_general x8, matrix products, per_device(): jnp.einsum('bhgus,buhgd->bshd', probabilities, grad_grouped, preferred_el...  11.6 us
    unnamed x113, local copies, waits for them, and re-layouts  10.4 us
    dot_general x8, matrix products, per_device(): jnp.einsum('bhgus,bshd->buhgd', probabilities, entry[1], preferred_elemen...  6.63 us
    psum x1, blocking collectives, per_device(): dot_total = lax.psum(jnp.sum(scaled_grad * attn_wide, axis=(2, 3)), 'head')  6.02 us
    dot_general x8, matrix products, per_device(): jnp.einsum('buhgd,bshd->bhgus', grad_grouped, value_block, preferred_elem...  5.83 us
    all_gather x1, blocking collectives, per_device(): lax.all_gather(jnp.sum(attn_wide * attn_wide, axis=(2, 3)), 'head')  4.79 us
  transfers between devices with their start and end apart: 28, of which 11 were waited for; matrix products, arithmetic and copies ran while one was open for 10% of the time, Pallas kernels for 0%

profile of v1, /device:TPU:227, one launch (start us, length us, event | category | flops | bytes accessed | tf_op | source)
XLA Modules:
  0.0 223.0 jit_solution(9300986127555297348)
XLA Ops:
  2.4 3.7 %collective-permute-start.13 = (bf16[1,256,2,128]{1,3,2,0:T(8,128)(2,1)}, bf16[1,256,2,128]{1,3,2,0:T(8,128)(2,1)S(1)}, u32[]{:S(2)}, u32[]{:S(2)}) collective-permute-start(bf16[1,256,2,128]{1,3,2,0:T(8,128)(2,1)} %copy.222), channel_id=1, source_target_pairs={{0,128},{2,130},{4,132},{6,134},{8,136},{10,138},{12,140},{14,142}... | collective-permute-start | bytes 393224 | tf_op jit(solution)/shard_map/ppermute | solution.py:13
  8.1 2.4 %collective-permute-start.11 = (bf16[1,256,2,128]{1,3,2,0:T(8,128)(2,1)}, bf16[1,256,2,128]{1,3,2,0:T(8,128)(2,1)S(1)}, u32[]{:S(2)}, u32[]{:S(2)}) collective-permute-start(bf16[1,256,2,128]{1,3,2,0:T(8,128)(2,1)} %copy.222), channel_id=1, source_target_pairs={{0,32},{2,34},{4,36},{6,38},{8,40},{10,42},{12,44},{14,46},{16,48}... | collective-permute-start | bytes 393224 | tf_op jit(solution)/shard_map/ppermute | solution.py:13
  10.5 5.2 %collective-permute-start.10 = (bf16[1,256,2,128]{1,3,2,0:T(8,128)(2,1)}, bf16[1,256,2,128]{1,3,2,0:T(8,128)(2,1)}, u32[]{:S(2)}, u32[]{:S(2)}) collective-permute-start(bf16[1,256,2,128]{1,3,2,0:T(8,128)(2,1)} %copy.222), channel_id=1, source_target_pairs={{0,16},{2,18},{4,20},{6,22},{8,24},{10,26},{12,28},{14,30},{16,32}... | collective-permute-start | bytes 393224 | tf_op jit(solution)/shard_map/ppermute | solution.py:13
  16.7 4.6 %collective-permute-start = (bf16[1,256,2,128]{3,1,2,0:T(8,128)(2,1)S(1)}, bf16[1,256,2,128]{3,1,2,0:T(8,128)(2,1)S(1)}, u32[]{:S(2)}, u32[]{:S(2)}) collective-permute-start(bf16[1,256,2,128]{3,1,2,0:T(8,128)(2,1)S(1)} %copy.206), channel_id=1, source_target_pairs={{0,2},{2,4},{4,6},{6,8},{8,10},{10,12},{12,14},{14,16},{16,18},{18... | collective-permute-start | bytes 393224 | tf_op jit(solution)/shard_map/ppermute | solution.py:13
  28.1 2.5 %collective-permute-start.1 = (bf16[1,256,2,128]{3,1,2,0:T(8,128)(2,1)S(1)}, bf16[1,256,2,128]{3,1,2,0:T(8,128)(2,1)S(1)}, u32[]{:S(2)}, u32[]{:S(2)}) collective-permute-start(bf16[1,256,2,128]{3,1,2,0:T(8,128)(2,1)S(1)} %copy.206), channel_id=1, source_target_pairs={{0,4},{2,6},{4,8},{6,10},{8,12},{10,14},{12,16},{14,18},{16,20},{1... | collective-permute-start | bytes 393224 | tf_op jit(solution)/shard_map/ppermute | solution.py:13
  31.1 4.3 %collective-permute-done.1 = bf16[1,256,2,128]{3,1,2,0:T(8,128)(2,1)S(1)} collective-permute-done((bf16[1,256,2,128]{3,1,2,0:T(8,128)(2,1)S(1)}, bf16[1,256,2,128]{3,1,2,0:T(8,128)(2,1)S(1)}, u32[]{:S(2)}, u32[]{:S(2)}) %collective-permute-start.1) | collective-permute-done | bytes 131104 | tf_op jit(solution)/shard_map/ppermute | solution.py:13
  35.4 4.5 %collective-permute-start.2 = (bf16[1,256,2,128]{3,1,2,0:T(8,128)(2,1)S(1)}, bf16[1,256,2,128]{3,1,2,0:T(8,128)(2,1)S(1)}, u32[]{:S(2)}, u32[]{:S(2)}) collective-permute-start(bf16[1,256,2,128]{3,1,2,0:T(8,128)(2,1)S(1)} %copy.206), channel_id=1, source_target_pairs={{0,8},{2,10},{4,12},{6,14},{8,16},{10,18},{12,20},{14,22},{16,24},... | collective-permute-start | bytes 393224 | tf_op jit(solution)/shard_map/ppermute | solution.py:13
  40.4 2.0 collective-permute-done.2
  42.3 3.0 %collective-permute-start.3 = (bf16[1,256,2,128]{3,1,2,0:T(8,128)(2,1)S(1)}, bf16[1,256,2,128]{3,1,2,0:T(8,128)(2,1)S(1)}, u32[]{:S(2)}, u32[]{:S(2)}) collective-permute-start(bf16[1,256,2,128]{3,1,2,0:T(8,128)(2,1)S(1)} %copy.206), channel_id=1, source_target_pairs={{0,16},{2,18},{4,20},{6,22},{8,24},{10,26},{12,28},{14,30},{16,32}... | collective-permute-start | bytes 393224 | tf_op jit(solution)/shard_map/ppermute | solution.py:13
  45.8 5.2 %collective-permute-done.3 = bf16[1,256,2,128]{3,1,2,0:T(8,128)(2,1)S(1)} collective-permute-done((bf16[1,256,2,128]{3,1,2,0:T(8,128)(2,1)S(1)}, bf16[1,256,2,128]{3,1,2,0:T(8,128)(2,1)S(1)}, u32[]{:S(2)}, u32[]{:S(2)}) %collective-permute-start.3) | collective-permute-done | bytes 131104 | tf_op jit(solution)/shard_map/ppermute | solution.py:13
  53.4 9.1 %collective-permute-done.4 = bf16[1,256,2,128]{3,1,2,0:T(8,128)(2,1)S(1)} collective-permute-done((bf16[1,256,2,128]{3,1,2,0:T(8,128)(2,1)S(1)}, bf16[1,256,2,128]{3,1,2,0:T(8,128)(2,1)S(1)}, u32[]{:S(2)}, u32[]{:S(2)}) %collective-permute-start.4) | collective-permute-done | bytes 131104 | tf_op jit(solution)/shard_map/ppermute | solution.py:13
  64.9 3.3 %collective-permute-done.5 = bf16[1,256,2,128]{3,1,2,0:T(8,128)(2,1)S(1)} collective-permute-done((bf16[1,256,2,128]{3,1,2,0:T(8,128)(2,1)S(1)}, bf16[1,256,2,128]{3,1,2,0:T(8,128)(2,1)S(1)}, u32[]{:S(2)}, u32[]{:S(2)}) %collective-permute-start.5) | collective-permute-done | bytes 131104 | tf_op jit(solution)/shard_map/ppermute | solution.py:13
  71.4 7.9 %collective-permute-start.7 = (bf16[1,256,2,128]{1,3,2,0:T(8,128)(2,1)}, bf16[1,256,2,128]{1,3,2,0:T(8,128)(2,1)S(1)}, u32[]{:S(2)}, u32[]{:S(2)}) collective-permute-start(bf16[1,256,2,128]{1,3,2,0:T(8,128)(2,1)} %copy.222), channel_id=1, source_target_pairs={{0,2},{2,4},{4,6},{6,8},{8,10},{10,12},{12,14},{14,16},{16,18},{18... | collective-permute-start | bytes 393224 | tf_op jit(solution)/shard_map/ppermute | solution.py:13
  82.9 11.9 %collective-permute-start.9 = (bf16[1,256,2,128]{1,3,2,0:T(8,128)(2,1)}, bf16[1,256,2,128]{1,3,2,0:T(8,128)(2,1)S(1)}, u32[]{:S(2)}, u32[]{:S(2)}) collective-permute-start(bf16[1,256,2,128]{1,3,2,0:T(8,128)(2,1)} %copy.222), channel_id=1, source_target_pairs={{0,8},{2,10},{4,12},{6,14},{8,16},{10,18},{12,20},{14,22},{16,24},... | collective-permute-start | bytes 393224 | tf_op jit(solution)/shard_map/ppermute | solution.py:13
  97.1 4.2 %collective-permute-start.8 = (bf16[1,256,2,128]{1,3,2,0:T(8,128)(2,1)}, bf16[1,256,2,128]{1,3,2,0:T(8,128)(2,1)S(1)}, u32[]{:S(2)}, u32[]{:S(2)}) collective-permute-start(bf16[1,256,2,128]{1,3,2,0:T(8,128)(2,1)} %copy.222), channel_id=1, source_target_pairs={{0,4},{2,6},{4,8},{6,10},{8,12},{10,14},{12,16},{14,18},{16,20},{1... | collective-permute-start | bytes 393224 | tf_op jit(solution)/shard_map/ppermute | solution.py:13
  105.6 2.2 fusion.100
  107.8 2.6 %copy.236 = f32[1,256,8,128]{3,2,1,0:T(8,128)} copy(f32[1,256,8,128]{1,3,2,0:T(8,128)} %bitcast.792) | data formatting | bytes 2097152 | tf_op jit(solution)/shard_map/convert_element_type | solution.py:74
  110.4 2.3 %multiply_reduce_fusion.1 = f32[256]{0:T(256)S(1)} fusion(f32[1,256,8,128]{3,2,1,0:T(8,128)} %copy.236, bf16[1,256,8,128]{3,2,1,0:T(8,128)(2,1)S(1)} %copy-done.19, f32[8,128]{1,0:T(8,128)S(1)} %copy-done.53), kind=kLoop, calls=%fused_computation.162 | loop fusion | flops 1048320 | bytes 1577984 | tf_op jit(solution)/shard_map/reduce_sum | solution.py:81
  112.7 6.0 %psum.7 = f32[1,256]{1,0:T(1,128)} all-reduce(f32[1,256]{1,0:T(1,128)S(1)} %bitcast.833), channel_id=1, replica_groups=mesh['seq'=128,'head'=2] {'head'}, use_global_device_ids=true, to_apply=%region_19.20 | all-reduce | flops 256 | bytes 2048 | tf_op jit(solution)/shard_map/psum | solution.py:81
  118.7 4.8 %all-gather.1 = f32[2,1,256]{2,1,0:T(1,128)S(1)} all-gather(f32[1,1,256]{2,1,0:T(1,128)} %bitcast.831), channel_id=2, replica_groups=mesh['seq'=128,'head'=2] {'head'}, dimensions={0}, use_global_device_ids=true | all-gather | bytes 3072 | tf_op jit(solution)/shard_map/all_gather | solution.py:76
  125.4 4.0 %multiply_reduce_fusion = (f32[256,8]{1,0:T(8,128)}, bf16[1,256,8,128]{3,2,1,0:T(8,128)(2,1)}, bf16[1,256,8,128]{3,2,1,0:T(8,128)(2,1)}) fusion(f32[1,256,8,128]{3,2,1,0:T(8,128)} %copy.236, f32[256]{0:T(256)S(1)} %bitcast.832, f32[256]{0:T(256)S(1)} %add_rsqrt_fusion, bf16[1,256,8,128]{3,2,1,0:T(8,128)(2,1)S(1)} %copy-done.19, f32[8,128]{1,0:T(8,128)S(1)} %copy-done.53), kind=kLoop, calls=%fused_computation.160 | loop fusion | flops 3143680 | bytes 2635776 | tf_op jit(solution)/shard_map/reduce_sum | solution.py:86
  130.8 2.9 %fusion.78 = bf16[1,256,2,128]{1,3,2,0:T(8,128)(2,1)} fusion(bf16[256,2,4,128]{0,3,2,1:T(8,128)(2,1)S(1)} %copy.282, f32[1,2,4,256,256]{3,4,2,1,0:T(8,128)} %copy-done.6, f32[2,4,256]{2,1,0:T(4,128)S(1)} %bitcast.776), kind=kOutput, calls=%fused_computation.136 | convolution fusion | flops 135331840 | bytes 2760704 | tf_op jit(solution)/shard_map/bhgus,buhgd->bshd/dot_general | solution.py:107
  133.7 2.9 %fusion.79 = bf16[1,256,2,128]{1,3,2,0:T(8,128)(2,1)} fusion(bf16[256,2,4,128]{0,3,2,1:T(8,128)(2,1)S(1)} %copy.282, f32[2,256,256,4]{2,1,3,0:T(8,128)} %copy-done.14, f32[2,4,256]{2,1,0:T(4,128)S(1)} %bitcast.777), kind=kOutput, calls=%fused_computation.137 | convolution fusion | flops 135331840 | bytes 2760704 | tf_op jit(solution)/shard_map/bhgus,buhgd->bshd/dot_general | solution.py:107
  154.7 2.1 collective-permute-start.14
  156.9 2.7 %collective-permute-start.21 = (bf16[1,256,2,128]{1,3,2,0:T(8,128)(2,1)S(1)}, bf16[1,256,2,128]{1,3,2,0:T(8,128)(2,1)S(1)}, u32[]{:S(2)}, u32[]{:S(2)}) collective-permute-start(bf16[1,256,2,128]{1,3,2,0:T(8,128)(2,1)S(1)} %copy-done.51), channel_id=1, source_target_pairs={{4,0},{6,2},{8,4},{10,6},{12,8},{14,10},{16,12},{18,14},{20,16},{2... | collective-permute-start | bytes 393224 | tf_op jit(solution)/shard_map/ppermute | solution.py:13
  163.4 2.1 collective-permute-start.16
  173.2 6.8 %collective-permute-start.17 = (bf16[1,256,2,128]{3,1,2,0:T(8,128)(2,1)S(1)}, bf16[1,256,2,128]{3,1,2,0:T(8,128)(2,1)S(1)}, u32[]{:S(2)}, u32[]{:S(2)}) collective-permute-start(bf16[1,256,2,128]{3,1,2,0:T(8,128)(2,1)S(1)} %fusion.88), channel_id=1, source_target_pairs={{32,0},{34,2},{36,4},{38,6},{40,8},{42,10},{44,12},{46,14},{48,16}... | collective-permute-start | bytes 393224 | tf_op jit(solution)/shard_map/ppermute | solution.py:13
  183.2 11.3 %collective-permute-start.20 = (bf16[1,256,2,128]{3,1,2,0:T(8,128)(2,1)S(1)}, bf16[1,256,2,128]{3,1,2,0:T(8,128)(2,1)S(1)}, u32[]{:S(2)}, u32[]{:S(2)}) collective-permute-start(bf16[1,256,2,128]{3,1,2,0:T(8,128)(2,1)S(1)} %fusion.85), channel_id=1, source_target_pairs={{2,0},{4,2},{6,4},{8,6},{10,8},{12,10},{14,12},{16,14},{18,16},{20... | collective-permute-start | bytes 393224 | tf_op jit(solution)/shard_map/ppermute | solution.py:13
  195.0 4.3 %collective-permute-start.23 = (bf16[1,256,2,128]{1,3,2,0:T(8,128)(2,1)S(1)}, bf16[1,256,2,128]{1,3,2,0:T(8,128)(2,1)S(1)}, u32[]{:S(2)}, u32[]{:S(2)}) collective-permute-start(bf16[1,256,2,128]{1,3,2,0:T(8,128)(2,1)S(1)} %fusion.82), channel_id=1, source_target_pairs={{16,0},{18,2},{20,4},{22,6},{24,8},{26,10},{28,12},{30,14},{32,16}... | collective-permute-start | bytes 393224 | tf_op jit(solution)/shard_map/ppermute | solution.py:13
  204.5 2.2 collective-permute-start.27
  208.3 5.2 %collective-permute-done.24 = bf16[1,256,2,128]{1,3,2,0:T(8,128)(2,1)S(1)} collective-permute-done((bf16[1,256,2,128]{1,3,2,0:T(8,128)(2,1)S(1)}, bf16[1,256,2,128]{1,3,2,0:T(8,128)(2,1)S(1)}, u32[]{:S(2)}, u32[]{:S(2)}) %collective-permute-start.24) | collective-permute-done | bytes 131104 | tf_op jit(solution)/shard_map/ppermute | solution.py:13
  214.3 7.3 %collective-permute-done.26 = bf16[1,256,2,128]{1,3,2,0:T(8,128)(2,1)S(1)} collective-permute-done((bf16[1,256,2,128]{1,3,2,0:T(8,128)(2,1)S(1)}, bf16[1,256,2,128]{1,3,2,0:T(8,128)(2,1)S(1)}, u32[]{:S(2)}, u32[]{:S(2)}) %collective-permute-start.26) | collective-permute-done | bytes 131104 | tf_op jit(solution)/shard_map/ppermute | solution.py:13
  (206 shorter events, 71.2 us)
Async XLA Ops:
  2.4 101.9 %collective-permute-start.13 = (bf16[1,256,2,128]{1,3,2,0:T(8,128)(2,1)}, bf16[1,256,2,128]{1,3,2,0:T(8,128)(2,1)S(1)}, u32[]{:S(2)}, u32[]{:S(2)}) collective-permute-start(bf16[1,256,2,128]{1,3,2,0:T(8,128)(2,1)} %copy.222), channel_id=1, source_target_pairs={{0,128},{2,130},{4,132},{6,134},{8,136},{10,138},{12,140},{14,142}... | collective-permute-start | bytes 393224 | tf_op jit(solution)/shard_map/ppermute | solution.py:13
  6.2 97.6 %collective-permute-start.12 = (bf16[1,256,2,128]{1,3,2,0:T(8,128)(2,1)}, bf16[1,256,2,128]{1,3,2,0:T(8,128)(2,1)S(1)}, u32[]{:S(2)}, u32[]{:S(2)}) collective-permute-start(bf16[1,256,2,128]{1,3,2,0:T(8,128)(2,1)} %copy.222), channel_id=1, source_target_pairs={{0,64},{2,66},{4,68},{6,70},{8,72},{10,74},{12,76},{14,78},{16,80}... | collective-permute-start | bytes 393224 | tf_op jit(solution)/shard_map/ppermute | solution.py:13
  8.1 95.1 %collective-permute-start.11 = (bf16[1,256,2,128]{1,3,2,0:T(8,128)(2,1)}, bf16[1,256,2,128]{1,3,2,0:T(8,128)(2,1)S(1)}, u32[]{:S(2)}, u32[]{:S(2)}) collective-permute-start(bf16[1,256,2,128]{1,3,2,0:T(8,128)(2,1)} %copy.222), channel_id=1, source_target_pairs={{0,32},{2,34},{4,36},{6,38},{8,40},{10,42},{12,44},{14,46},{16,48}... | collective-permute-start | bytes 393224 | tf_op jit(solution)/shard_map/ppermute | solution.py:13
  10.5 91.2 %collective-permute-start.10 = (bf16[1,256,2,128]{1,3,2,0:T(8,128)(2,1)}, bf16[1,256,2,128]{1,3,2,0:T(8,128)(2,1)}, u32[]{:S(2)}, u32[]{:S(2)}) collective-permute-start(bf16[1,256,2,128]{1,3,2,0:T(8,128)(2,1)} %copy.222), channel_id=1, source_target_pairs={{0,16},{2,18},{4,20},{6,22},{8,24},{10,26},{12,28},{14,30},{16,32}... | collective-permute-start | bytes 393224 | tf_op jit(solution)/shard_map/ppermute | solution.py:13
  16.7 11.4 %collective-permute-start = (bf16[1,256,2,128]{3,1,2,0:T(8,128)(2,1)S(1)}, bf16[1,256,2,128]{3,1,2,0:T(8,128)(2,1)S(1)}, u32[]{:S(2)}, u32[]{:S(2)}) collective-permute-start(bf16[1,256,2,128]{3,1,2,0:T(8,128)(2,1)S(1)} %copy.206), channel_id=1, source_target_pairs={{0,2},{2,4},{4,6},{6,8},{8,10},{10,12},{12,14},{14,16},{16,18},{18... | collective-permute-start | bytes 393224 | tf_op jit(solution)/shard_map/ppermute | solution.py:13
  22.8 57.1 %copy-start.44 = (f32[2,4,256]{2,1,0:T(4,128)}, f32[2,4,256]{2,1,0:T(4,128)S(1)}, u32[]{:S(2)}) copy-start(f32[2,4,256]{2,1,0:T(4,128)S(1)} %get-tuple-element.44) | copy-start | bytes 24580
  28.1 7.3 %collective-permute-start.1 = (bf16[1,256,2,128]{3,1,2,0:T(8,128)(2,1)S(1)}, bf16[1,256,2,128]{3,1,2,0:T(8,128)(2,1)S(1)}, u32[]{:S(2)}, u32[]{:S(2)}) collective-permute-start(bf16[1,256,2,128]{3,1,2,0:T(8,128)(2,1)S(1)} %copy.206), channel_id=1, source_target_pairs={{0,4},{2,6},{4,8},{6,10},{8,12},{10,14},{12,16},{14,18},{16,20},{1... | collective-permute-start | bytes 393224 | tf_op jit(solution)/shard_map/ppermute | solution.py:13
  31.1 63.7 %copy-start.6 = (f32[1,2,4,256,256]{3,4,2,1,0:T(8,128)}, f32[1,2,4,256,256]{3,4,2,1,0:T(8,128)S(1)}, u32[]{:S(2)}) copy-start(f32[1,2,4,256,256]{3,4,2,1,0:T(8,128)S(1)} %get-tuple-element.47) | copy-start | bytes 6291460
  35.4 7.0 %collective-permute-start.2 = (bf16[1,256,2,128]{3,1,2,0:T(8,128)(2,1)S(1)}, bf16[1,256,2,128]{3,1,2,0:T(8,128)(2,1)S(1)}, u32[]{:S(2)}, u32[]{:S(2)}) collective-permute-start(bf16[1,256,2,128]{3,1,2,0:T(8,128)(2,1)S(1)} %copy.206), channel_id=1, source_target_pairs={{0,8},{2,10},{4,12},{6,14},{8,16},{10,18},{12,20},{14,22},{16,24},... | collective-permute-start | bytes 393224 | tf_op jit(solution)/shard_map/ppermute | solution.py:13
  40.4 64.4 %copy-start.16 = (f32[2,256,256,4]{2,1,3,0:T(8,128)}, f32[2,256,256,4]{2,1,3,0:T(8,128)S(1)}, u32[]{:S(2)}) copy-start(f32[2,256,256,4]{2,1,3,0:T(8,128)S(1)} %get-tuple-element.43) | copy-start | bytes 6291460
  42.3 8.7 %collective-permute-start.3 = (bf16[1,256,2,128]{3,1,2,0:T(8,128)(2,1)S(1)}, bf16[1,256,2,128]{3,1,2,0:T(8,128)(2,1)S(1)}, u32[]{:S(2)}, u32[]{:S(2)}) collective-permute-start(bf16[1,256,2,128]{3,1,2,0:T(8,128)(2,1)S(1)} %copy.206), channel_id=1, source_target_pairs={{0,16},{2,18},{4,20},{6,22},{8,24},{10,26},{12,28},{14,30},{16,32}... | collective-permute-start | bytes 393224 | tf_op jit(solution)/shard_map/ppermute | solution.py:13
  45.8 55.4 %copy-start.8 = (f32[2,256,256,4]{2,1,3,0:T(8,128)}, f32[2,256,256,4]{2,1,3,0:T(8,128)S(1)}, u32[]{:S(2)}) copy-start(f32[2,256,256,4]{2,1,3,0:T(8,128)S(1)} %get-tuple-element.41) | copy-start | bytes 6291460
  51.0 11.5 %collective-permute-start.4 = (bf16[1,256,2,128]{3,1,2,0:T(8,128)(2,1)S(1)}, bf16[1,256,2,128]{3,1,2,0:T(8,128)(2,1)S(1)}, u32[]{:S(2)}, u32[]{:S(2)}) collective-permute-start(bf16[1,256,2,128]{3,1,2,0:T(8,128)(2,1)S(1)} %copy.206), channel_id=1, source_target_pairs={{0,32},{2,34},{4,36},{6,38},{8,40},{10,42},{12,44},{14,46},{16,48}... | collective-permute-start | bytes 393224 | tf_op jit(solution)/shard_map/ppermute | solution.py:13
  62.5 5.7 %collective-permute-start.5 = (bf16[1,256,2,128]{3,1,2,0:T(8,128)(2,1)S(1)}, bf16[1,256,2,128]{3,1,2,0:T(8,128)(2,1)S(1)}, u32[]{:S(2)}, u32[]{:S(2)}) collective-permute-start(bf16[1,256,2,128]{3,1,2,0:T(8,128)(2,1)S(1)} %copy.206), channel_id=1, source_target_pairs={{0,64},{2,66},{4,68},{6,70},{8,72},{10,74},{12,76},{14,78},{16,80}... | collective-permute-start | bytes 393224 | tf_op jit(solution)/shard_map/ppermute | solution.py:13
  68.2 3.2 %collective-permute-start.6 = (bf16[1,256,2,128]{3,1,2,0:T(8,128)(2,1)S(1)}, bf16[1,256,2,128]{3,1,2,0:T(8,128)(2,1)S(1)}, u32[]{:S(2)}, u32[]{:S(2)}) collective-permute-start(bf16[1,256,2,128]{3,1,2,0:T(8,128)(2,1)S(1)} %copy.206), channel_id=1, source_target_pairs={{0,128},{2,130},{4,132},{6,134},{8,136},{10,138},{12,140},{14,142}... | collective-permute-start | bytes 393224 | tf_op jit(solution)/shard_map/ppermute | solution.py:13
  71.4 11.5 %collective-permute-start.7 = (bf16[1,256,2,128]{1,3,2,0:T(8,128)(2,1)}, bf16[1,256,2,128]{1,3,2,0:T(8,128)(2,1)S(1)}, u32[]{:S(2)}, u32[]{:S(2)}) collective-permute-start(bf16[1,256,2,128]{1,3,2,0:T(8,128)(2,1)} %copy.222), channel_id=1, source_target_pairs={{0,2},{2,4},{4,6},{6,8},{8,10},{10,12},{12,14},{14,16},{16,18},{18... | collective-permute-start | bytes 393224 | tf_op jit(solution)/shard_map/ppermute | solution.py:13
  82.9 14.2 %collective-permute-start.9 = (bf16[1,256,2,128]{1,3,2,0:T(8,128)(2,1)}, bf16[1,256,2,128]{1,3,2,0:T(8,128)(2,1)S(1)}, u32[]{:S(2)}, u32[]{:S(2)}) collective-permute-start(bf16[1,256,2,128]{1,3,2,0:T(8,128)(2,1)} %copy.222), channel_id=1, source_target_pairs={{0,8},{2,10},{4,12},{6,14},{8,16},{10,18},{12,20},{14,22},{16,24},... | collective-permute-start | bytes 393224 | tf_op jit(solution)/shard_map/ppermute | solution.py:13
  97.1 7.8 %collective-permute-start.8 = (bf16[1,256,2,128]{1,3,2,0:T(8,128)(2,1)}, bf16[1,256,2,128]{1,3,2,0:T(8,128)(2,1)S(1)}, u32[]{:S(2)}, u32[]{:S(2)}) collective-permute-start(bf16[1,256,2,128]{1,3,2,0:T(8,128)(2,1)} %copy.222), channel_id=1, source_target_pairs={{0,4},{2,6},{4,8},{6,10},{8,12},{10,14},{12,16},{14,18},{16,20},{1... | collective-permute-start | bytes 393224 | tf_op jit(solution)/shard_map/ppermute | solution.py:13
  154.7 18.5 %collective-permute-start.14 = (bf16[1,256,2,128]{3,1,2,0:T(8,128)(2,1)S(1)}, bf16[1,256,2,128]{3,1,2,0:T(8,128)(2,1)S(1)}, u32[]{:S(2)}, u32[]{:S(2)}) collective-permute-start(bf16[1,256,2,128]{3,1,2,0:T(8,128)(2,1)S(1)} %fusion.91), channel_id=1, source_target_pairs={{4,0},{6,2},{8,4},{10,6},{12,8},{14,10},{16,12},{18,14},{20,16},{2... | collective-permute-start | bytes 393224 | tf_op jit(solution)/shard_map/ppermute | solution.py:13
  156.9 23.1 %collective-permute-start.21 = (bf16[1,256,2,128]{1,3,2,0:T(8,128)(2,1)S(1)}, bf16[1,256,2,128]{1,3,2,0:T(8,128)(2,1)S(1)}, u32[]{:S(2)}, u32[]{:S(2)}) collective-permute-start(bf16[1,256,2,128]{1,3,2,0:T(8,128)(2,1)S(1)} %copy-done.51), channel_id=1, source_target_pairs={{4,0},{6,2},{8,4},{10,6},{12,8},{14,10},{16,12},{18,14},{20,16},{2... | collective-permute-start | bytes 393224 | tf_op jit(solution)/shard_map/ppermute | solution.py:13
  159.6 22.3 %collective-permute-start.15 = (bf16[1,256,2,128]{3,1,2,0:T(8,128)(2,1)S(1)}, bf16[1,256,2,128]{3,1,2,0:T(8,128)(2,1)S(1)}, u32[]{:S(2)}, u32[]{:S(2)}) collective-permute-start(bf16[1,256,2,128]{3,1,2,0:T(8,128)(2,1)S(1)} %fusion.90), channel_id=1, source_target_pairs={{8,0},{10,2},{12,4},{14,6},{16,8},{18,10},{20,12},{22,14},{24,16},... | collective-permute-start | bytes 393224 | tf_op jit(solution)/shard_map/ppermute | solution.py:13
  161.5 21.7 %collective-permute-start.22 = (bf16[1,256,2,128]{1,3,2,0:T(8,128)(2,1)S(1)}, bf16[1,256,2,128]{1,3,2,0:T(8,128)(2,1)S(1)}, u32[]{:S(2)}, u32[]{:S(2)}) collective-permute-start(bf16[1,256,2,128]{1,3,2,0:T(8,128)(2,1)S(1)} %copy-done.50), channel_id=1, source_target_pairs={{8,0},{10,2},{12,4},{14,6},{16,8},{18,10},{20,12},{22,14},{24,16},... | collective-permute-start | bytes 393224 | tf_op jit(solution)/shard_map/ppermute | solution.py:13
  163.4 31.5 %collective-permute-start.16 = (bf16[1,256,2,128]{3,1,2,0:T(8,128)(2,1)S(1)}, bf16[1,256,2,128]{3,1,2,0:T(8,128)(2,1)S(1)}, u32[]{:S(2)}, u32[]{:S(2)}) collective-permute-start(bf16[1,256,2,128]{3,1,2,0:T(8,128)(2,1)S(1)} %fusion.89), channel_id=1, source_target_pairs={{16,0},{18,2},{20,4},{22,6},{24,8},{26,10},{28,12},{30,14},{32,16}... | collective-permute-start | bytes 393224 | tf_op jit(solution)/shard_map/ppermute | solution.py:13
  173.2 26.1 %collective-permute-start.17 = (bf16[1,256,2,128]{3,1,2,0:T(8,128)(2,1)S(1)}, bf16[1,256,2,128]{3,1,2,0:T(8,128)(2,1)S(1)}, u32[]{:S(2)}, u32[]{:S(2)}) collective-permute-start(bf16[1,256,2,128]{3,1,2,0:T(8,128)(2,1)S(1)} %fusion.88), channel_id=1, source_target_pairs={{32,0},{34,2},{36,4},{38,6},{40,8},{42,10},{44,12},{46,14},{48,16}... | collective-permute-start | bytes 393224 | tf_op jit(solution)/shard_map/ppermute | solution.py:13
  179.9 21.3 %collective-permute-start.18 = (bf16[1,256,2,128]{3,1,2,0:T(8,128)(2,1)S(1)}, bf16[1,256,2,128]{3,1,2,0:T(8,128)(2,1)S(1)}, u32[]{:S(2)}, u32[]{:S(2)}) collective-permute-start(bf16[1,256,2,128]{3,1,2,0:T(8,128)(2,1)S(1)} %fusion.87), channel_id=1, source_target_pairs={{64,0},{66,2},{68,4},{70,6},{72,8},{74,10},{76,12},{78,14},{80,16}... | collective-permute-start | bytes 393224 | tf_op jit(solution)/shard_map/ppermute | solution.py:13
  181.9 21.3 %collective-permute-start.19 = (bf16[1,256,2,128]{3,1,2,0:T(8,128)(2,1)S(1)}, bf16[1,256,2,128]{3,1,2,0:T(8,128)(2,1)S(1)}, u32[]{:S(2)}, u32[]{:S(2)}) collective-permute-start(bf16[1,256,2,128]{3,1,2,0:T(8,128)(2,1)S(1)} %fusion.86), channel_id=1, source_target_pairs={{128,0},{130,2},{132,4},{134,6},{136,8},{138,10},{140,12},{142,14}... | collective-permute-start | bytes 393224 | tf_op jit(solution)/shard_map/ppermute | solution.py:13
  183.2 21.3 %collective-permute-start.20 = (bf16[1,256,2,128]{3,1,2,0:T(8,128)(2,1)S(1)}, bf16[1,256,2,128]{3,1,2,0:T(8,128)(2,1)S(1)}, u32[]{:S(2)}, u32[]{:S(2)}) collective-permute-start(bf16[1,256,2,128]{3,1,2,0:T(8,128)(2,1)S(1)} %fusion.85), channel_id=1, source_target_pairs={{2,0},{4,2},{6,4},{8,6},{10,8},{12,10},{14,12},{16,14},{18,16},{20... | collective-permute-start | bytes 393224 | tf_op jit(solution)/shard_map/ppermute | solution.py:13
  195.0 13.3 %collective-permute-start.23 = (bf16[1,256,2,128]{1,3,2,0:T(8,128)(2,1)S(1)}, bf16[1,256,2,128]{1,3,2,0:T(8,128)(2,1)S(1)}, u32[]{:S(2)}, u32[]{:S(2)}) collective-permute-start(bf16[1,256,2,128]{1,3,2,0:T(8,128)(2,1)S(1)} %fusion.82), channel_id=1, source_target_pairs={{16,0},{18,2},{20,4},{22,6},{24,8},{26,10},{28,12},{30,14},{32,16}... | collective-permute-start | bytes 393224 | tf_op jit(solution)/shard_map/ppermute | solution.py:13
  199.3 14.2 %collective-permute-start.24 = (bf16[1,256,2,128]{1,3,2,0:T(8,128)(2,1)S(1)}, bf16[1,256,2,128]{1,3,2,0:T(8,128)(2,1)S(1)}, u32[]{:S(2)}, u32[]{:S(2)}) collective-permute-start(bf16[1,256,2,128]{1,3,2,0:T(8,128)(2,1)S(1)} %copy-done.49), channel_id=1, source_target_pairs={{32,0},{34,2},{36,4},{38,6},{40,8},{42,10},{44,12},{46,14},{48,16}... | collective-permute-start | bytes 393224 | tf_op jit(solution)/shard_map/ppermute | solution.py:13
  201.3 13.0 %collective-permute-start.25 = (bf16[1,256,2,128]{1,3,2,0:T(8,128)(2,1)S(1)}, bf16[1,256,2,128]{1,3,2,0:T(8,128)(2,1)S(1)}, u32[]{:S(2)}, u32[]{:S(2)}) collective-permute-start(bf16[1,256,2,128]{1,3,2,0:T(8,128)(2,1)S(1)} %copy-done.48), channel_id=1, source_target_pairs={{64,0},{66,2},{68,4},{70,6},{72,8},{74,10},{76,12},{78,14},{80,16}... | collective-permute-start | bytes 393224 | tf_op jit(solution)/shard_map/ppermute | solution.py:13
  203.2 18.4 %collective-permute-start.26 = (bf16[1,256,2,128]{1,3,2,0:T(8,128)(2,1)S(1)}, bf16[1,256,2,128]{1,3,2,0:T(8,128)(2,1)S(1)}, u32[]{:S(2)}, u32[]{:S(2)}) collective-permute-start(bf16[1,256,2,128]{1,3,2,0:T(8,128)(2,1)S(1)} %copy-done.47), channel_id=1, source_target_pairs={{128,0},{130,2},{132,4},{134,6},{136,8},{138,10},{140,12},{142,14}... | collective-permute-start | bytes 393224 | tf_op jit(solution)/shard_map/ppermute | solution.py:13
  204.5 17.1 %collective-permute-start.27 = (bf16[1,256,2,128]{1,3,2,0:T(8,128)(2,1)S(1)}, bf16[1,256,2,128]{1,3,2,0:T(8,128)(2,1)S(1)}, u32[]{:S(2)}, u32[]{:S(2)}) collective-permute-start(bf16[1,256,2,128]{1,3,2,0:T(8,128)(2,1)S(1)} %copy-done.46), channel_id=1, source_target_pairs={{2,0},{4,2},{6,4},{8,6},{10,8},{12,10},{14,12},{16,14},{18,16},{20... | collective-permute-start | bytes 393224 | tf_op jit(solution)/shard_map/ppermute | solution.py:13
  (50 other events, 499.3 us)
